TPU v7x, 256 devices: a whole 4x4x8 slice. The times are simulated.
256 devices in a mesh: col: 64 (over z, x, core), row: 4 (over y).
Axes of the slice: x: 4, y: 4, z: 8, core: 2. Of those that a mesh axis runs over, the one named last changes fastest.
Arguments:
- matrix: float32 [16, 512, 1, 8192], P(None, 'row', None, 'col'), may hold values from -1 to 5, as said below
- inverse_factors: float32 [2, 512, 512], replicated, may hold values from -1 to 1, as said below
Outputs:
- factored: float32 [16, 512, 1, 8192], P(None, 'row', None, 'col')
Inputs may be any that keep to these rules, and one draw needn't show every extreme that they name: matrix holds a symmetric matrix. Each inverse_factors[k] is lower triangular with a positive diagonal; it is given independently of matrix.
All inputs are finite; a program needn't handle non-finite values.
Results may differ from a plain program's by a relative error of at most 0.0001.
Values sent between devices are 32-bit elements; how exact they have to be, the bound alone decides.
No kernel may reach another device: no remote copies, remote signals or barrier semaphores. Data moves between devices by JAX's collectives and lax.ppermute only.
A program may use at most 64 MiB of HBM per device.

v0:
```python
import jax
import jax.numpy as jnp
from jax import lax
from jax.sharding import PartitionSpec as P


def broadcast(x, axis, root):
    mine = lax.axis_index(axis) == root
    return lax.psum(jnp.where(mine, x, jnp.zeros_like(x)), axis)


def exact_dot(left_side, right_side):
    return jnp.dot(
        left_side, right_side, precision=lax.Precision.HIGHEST, preferred_element_type=jnp.float32
    )


def shards(matrix, inverse_factors):
    col_count = lax.axis_size("col")
    row_count = lax.axis_size("row")
    col_index = lax.axis_index("col")
    row_index = lax.axis_index("row")
    row_blocks, block_cols, cycles, _ = matrix.shape
    panel_width = inverse_factors.shape[1]
    per_panel = panel_width // block_cols
    local_rows = row_blocks * block_cols
    square_view = matrix.reshape(local_rows, cycles * block_cols)
    global_rows = (
        (jnp.arange(row_blocks)[:, None] * row_count + row_index) * block_cols
        + jnp.arange(block_cols)[None, :]
    ).reshape(-1)
    take_index = (jnp.arange(cycles) * col_count + col_index) // row_count
    row_root = col_index % row_count

    def masked(factor_cols, offset):
        return jnp.where(global_rows[:, None] >= offset, factor_cols, 0.0)

    current = square_view
    for panel in range(2):
        factor = inverse_factors[panel]
        pieces = [
            broadcast(current, "col", panel * per_panel + member) for member in range(per_panel)
        ]
        factor_cols = exact_dot(jnp.concatenate(pieces, axis=1), factor.T)
        trailing = masked(factor_cols, (panel + 1) * panel_width)
        blocked = trailing.reshape(row_blocks, block_cols, panel_width)
        picked = jnp.take(blocked, take_index, axis=0).reshape(cycles * block_cols, panel_width)
        gathered = lax.all_gather(picked, "row", axis=0, tiled=True)
        column_part = lax.dynamic_slice_in_dim(
            gathered, row_root * picked.shape[0], picked.shape[0], 0
        )
        current = current - exact_dot(trailing, column_part.T)
        place_factor_cols = masked(factor_cols, panel * panel_width)
        offset_id = col_index - panel * per_panel
        inside = (offset_id >= 0) & (offset_id < per_panel)
        position = jnp.clip(offset_id, 0, per_panel - 1)
        chosen = lax.dynamic_slice_in_dim(place_factor_cols, position * block_cols, block_cols, 1)
        leading = jnp.where(inside, chosen, current)
        current = jnp.concatenate([leading, current[:, block_cols:]], axis=1)
    return current.reshape(row_blocks, block_cols, cycles, block_cols)


def solution(mesh):
    return jax.shard_map(
        shards,
        mesh=mesh,
        in_specs=(P(None, "row", None, "col"), P()),
        out_specs=P(None, "row", None, "col"),
        check_vma=False,
    )
```

profile of v0, /device:TPU:2, one launch (start us, length us, event | category | flops | bytes accessed | tf_op | source)
XLA Modules:
  0.0 504.0 jit_solution(6828557385005431134)
XLA Ops:
  6.5 0.0 all-reduce.7.cloned.1.call-start
  6.5 0.0 copy-start.3
  6.5 3.4 broadcast_select_fusion.9
  10.0 0.0 all-reduce.7.cloned.1.call-update
  10.0 0.0 all-gather.5.cloned.1.call-start
  10.1 0.1 fusion.31
  10.2 199.4 %all-reduce.7.cloned.1.call-done = (f32[2048,128]{1,0:T(8,128)}, f32[2048,128]{1,0:T(8,128)}, f32[2048,128]{1,0:T(8,128)}, f32[2048,128]{1,0:T(8,128)}) async-done(((f32[2048,128]{1,0:T(8,128)}, f32[2048,128]{1,0:T(8,128)}, f32[2048,128]{1,0:T(8,128)}, f32[2048,128]{1,0:T(8,128)}), (f32[2048,128]{1,0:T(8,128)}, f32[2048,128]{1,0:T(8,128)}, f32[2048,128]{1,0:T(8,128)}, ...) | async-done | bytes 4194320 | tf_op jit(solution)/shard_map/psum | solution.py:9
  209.6 0.0 copy-done.3
  209.6 0.0 copy-start.2
  209.6 9.9 %broadcast_select_fusion = (f32[2048,512]{1,0:T(8,128)S(1)}, f32[2048,512]{1,0:T(8,128)}) fusion(pred[2048]{0:T(1024)(128)(4,1)S(1)} %get-tuple-element.35, f32[2,512,512]{2,1,0:T(8,128)S(1)} %copy-done.3, f32[2048,128]{1,0:T(8,128)} %get-tuple-element.21, f32[2048,128]{1,0:T(8,128)} %get-tuple-element.22, f32[2048,128]{1,0:T(8,128)} %get-tuple-element.23, ...), kind=kOutput, calls=%fused_computation.20 | convolution fusion | flops 6446645248 | bytes 13633536 | tf_op jit(solution)/shard_map/dot_general | solution.py:13
  219.5 0.0 copy-start
  219.5 2.0 copy-done
  221.5 0.7 dynamic-slice_select_fusion.3
  222.2 0.0 all-gather.5.cloned.1.call-update
  222.2 0.0 all-reduce.5.cloned.1.call-start
  222.3 25.7 %all-gather.5.cloned.1.call-done = f32[1,512,512]{2,1,0:T(8,128)} async-done(((f32[1,128,512]{2,1,0:T(8,128)}), f32[1,512,512]{2,1,0:T(8,128)}) %all-gather.5.cloned.1.call-update) | async-done | bytes 1048592 | tf_op jit(solution)/shard_map/all_gather | solution.py:48
  248.0 0.0 copy-done.2
  248.0 8.0 %broadcast_select_fusion.5 = (f32[2048,128]{1,0:T(8,128)}, f32[2048,128]{1,0:T(8,128)}, f32[2048,128]{1,0:T(8,128)}, f32[2048,128]{1,0:T(8,128)}, f32[2048,128]{1,0:T(8,128)S(1)}) fusion(pred[]{:T(512)S(6)} %eq.26, pred[]{:T(512)S(6)} %eq.33, pred[]{:T(512)S(6)} %eq.32, pred[]{:T(512)S(6)} %eq.31, f32[2048,128]{1,0:T(8,128)S(1)} %bitcast.40, ...), kind=kOutput, calls=%fused_computation.31 | convolution fusion | flops 1612447744 | bytes 11798541 | tf_op jit(solution)/shard_map/dot_general | solution.py:13
  256.0 0.0 all-reduce.5.cloned.1.call-update
  256.0 0.2 all-gather.7.cloned.1.call-start
  256.3 195.5 %all-reduce.5.cloned.1.call-done = (f32[2048,128]{1,0:T(8,128)}, f32[2048,128]{1,0:T(8,128)}, f32[2048,128]{1,0:T(8,128)}, f32[2048,128]{1,0:T(8,128)}) async-done(((f32[2048,128]{1,0:T(8,128)}, f32[2048,128]{1,0:T(8,128)}, f32[2048,128]{1,0:T(8,128)}, f32[2048,128]{1,0:T(8,128)}), (f32[2048,128]{1,0:T(8,128)}, f32[2048,128]{1,0:T(8,128)}, f32[2048,128]{1,0:T(8,128)}, ...) | async-done | bytes 4194320 | tf_op jit(solution)/shard_map/psum | solution.py:9
  451.7 10.3 %broadcast_select_fusion.1 = (f32[2048,512]{1,0:T(8,128)S(1)}, f32[2048,512]{1,0:T(8,128)}) fusion(pred[2048]{0:T(1024)(128)(4,1)S(1)} %get-tuple-element.33, f32[2,512,512]{2,1,0:T(8,128)} %param.5, f32[2048,128]{1,0:T(8,128)} %get-tuple-element.17, f32[2048,128]{1,0:T(8,128)} %get-tuple-element.18, f32[2048,128]{1,0:T(8,128)} %get-tuple-element.19, ...), kind=kOutput, calls=%fused_computation.21 | convolution fusion | flops 6446645248 | bytes 13633536 | tf_op jit(solution)/shard_map/dot_general | solution.py:13
  462.0 0.0 copy-start.1
  462.0 2.0 copy-done.1
  464.0 0.7 dynamic-slice_select_fusion.2
  464.7 0.0 all-gather.7.cloned.1.call-update
  464.8 25.7 %all-gather.7.cloned.1.call-done = f32[1,512,512]{2,1,0:T(8,128)} async-done(((f32[1,128,512]{2,1,0:T(8,128)}), f32[1,512,512]{2,1,0:T(8,128)}) %all-gather.7.cloned.1.call-update) | async-done | bytes 1048592 | tf_op jit(solution)/shard_map/all_gather | solution.py:48
  490.5 7.0 %fusion.16 = f32[2048,128]{1,0:T(8,128)} fusion(f32[2048,128]{1,0:T(8,128)S(1)} %get-tuple-element.38, f32[2048,512]{1,0:T(8,128)} %copy-done.1, f32[2048,512]{1,0:T(8,128)} %get-tuple-element.40, s32[]{:T(128)S(6)} %select_n.137, pred[2048]{0:T(1024)(128)(4,1)S(1)} %get-tuple-element.35, pred[]{:T(512)S(6)} %and.21, ...), kind=kOutput, calls=%fused_computation.17 | convolution fusion | flops 1611399168 | bytes 7604233 | tf_op jit(solution)/shard_map/dot_general | solution.py:13
  (1 shorter events, 0.0 us)
Async XLA Ops:
  6.5 203.1 %all-reduce.7.cloned.1.call-start = ((), (), s32[]{:S(2)}) async-start(), calls=%async_computation.3 | async-start | bytes 8388608 | tf_op jit(solution)/shard_map/psum | solution.py:9
  6.5 203.1 %copy-start.3 = (f32[2,512,512]{2,1,0:T(8,128)S(1)}, f32[2,512,512]{2,1,0:T(8,128)}, u32[]{:S(2)}) copy-start(f32[2,512,512]{2,1,0:T(8,128)} %param.5) | copy-start | bytes 6291460
  10.0 238.0 %all-gather.5.cloned.1.call-start = ((), (), s32[]{:S(2)}) async-start(), calls=%async_computation | async-start | bytes 1310720 | tf_op jit(solution)/shard_map/all_gather | solution.py:48
  209.6 38.4 %copy-start.2 = (f32[16,128,1,128]{3,2,1,0:T(1,128)S(1)}, f32[16,128,1,128]{3,2,1,0:T(1,128)}, u32[]{:S(2)}) copy-start(f32[16,128,1,128]{3,2,1,0:T(1,128)} %param.4) | copy-start | bytes 3145732
  219.5 2.0 copy-start
  222.2 229.5 %all-reduce.5.cloned.1.call-start = ((), (), s32[]{:S(2)}) async-start(), calls=%async_computation.2 | async-start | bytes 8388608 | tf_op jit(solution)/shard_map/psum | solution.py:9
  256.0 234.5 %all-gather.7.cloned.1.call-start = ((), (), s32[]{:S(2)}) async-start(), calls=%async_computation.1 | async-start | bytes 1310720 | tf_op jit(solution)/shard_map/all_gather | solution.py:48
  462.0 2.0 copy-start.1
Sparse Core Ops, SparseCore 0:
  11.3 198.2 all-reduce.6
  222.3 25.5 all-gather.4
  256.1 195.5 all-reduce.4
  464.9 25.5 all-gather.6
where the time goes:
time: 504 us
  waiting for transfers between devices  446 us (88%)
  matrix products  35.2 us (7%)
  between operations  13.2 us (3%)
    psum x2, waiting for transfers between devices, broadcast(): return lax.psum(jnp.where(mine, x, jnp.zeros_like(x)), axis)  395 us
    all_gather x2, waiting for transfers between devices, shards(): gathered = lax.all_gather(picked, 'row', axis=0, tiled=True)  51.4 us
    dot_general x4, matrix products, exact_dot(): jnp.dot(left_side, right_side, precision=lax.Precision.HIGHEST, preferred...  35.2 us
  transfers between devices with their start and end apart: 4, of which 4 were waited for; matrix products, arithmetic and copies ran while one was open for 0% of the time, Pallas kernels for 0%

commit v1 on v0

--- a/solution.py
+++ b/solution.py
@@ -45,7 +45,11 @@
         trailing = masked(factor_cols, (panel + 1) * panel_width)
         blocked = trailing.reshape(row_blocks, block_cols, panel_width)
         picked = jnp.take(blocked, take_index, axis=0).reshape(cycles * block_cols, panel_width)
-        gathered = lax.all_gather(picked, "row", axis=0, tiled=True)
+        devices = lax.axis_size("row")
+        repeats = [devices if d == 0 else 1 for d in range(picked.ndim)]
+        gathered = lax.all_to_all(
+            jnp.tile(picked, repeats), "row", split_axis=0, concat_axis=0, tiled=True
+        )
         column_part = lax.dynamic_slice_in_dim(
             gathered, row_root * picked.shape[0], picked.shape[0], 0
         )

time: 504 us -> 487 us (0.966)
  waiting for transfers between devices: 446 us -> 420 us
  starting transfers between devices: 0.31 us -> 8.57 us
    all_gather x2 -> x0, waiting for transfers between devices: 51.4 us -> none  [shards(): gathered = lax.all_gather(picked, 'row', axis=0, tiled=True)]
    all_to_all x0 -> x2, waiting for transfers between devices: none -> 27.4 us  [shards(): lax.all_to_all(jnp.tile(picked, repeats), 'row', split_axis=0, concat_axi...]
    all_to_all x0 -> x2, starting transfers between devices: none -> 8.57 us  [shards(): lax.all_to_all(jnp.tile(picked, repeats), 'row', split_axis=0, concat_axi...]
where the time goes in v1:
time: 487 us; the launch traced here: 486 us
  waiting for transfers between devices  420 us (86%)
  matrix products  35 us (7%)
  between operations  13.4 us (3%)
  starting transfers between devices  8.57 us (2%)
  local copies, waits for them, and re-layouts  6.16 us (1%)
    psum x2, waiting for transfers between devices, broadcast(): return lax.psum(jnp.where(mine, x, jnp.zeros_like(x)), axis)  392 us
    dot_general x4, matrix products, exact_dot(): jnp.dot(left_side, right_side, precision=lax.Precision.HIGHEST, preferred...  35 us
    all_to_all x2, waiting for transfers between devices, shards(): lax.all_to_all(jnp.tile(picked, repeats), 'row', split_axis=0, concat_axi...  27.4 us
  transfers between devices with their start and end apart: 4, of which 4 were waited for; matrix products, arithmetic and copies ran while one was open for 0% of the time, Pallas kernels for 0%

profile of v1, /device:TPU:2, one launch (start us, length us, event | category | flops | bytes accessed | tf_op | source)
XLA Modules:
  0.0 486.4 jit_solution(5711089034028160663)
XLA Ops:
  6.5 0.0 all-reduce.7.cloned.1.call-start
  6.5 0.0 copy-start.3
  6.5 3.4 broadcast_select_fusion.9
  10.0 0.0 all-reduce.7.cloned.1.call-update
  10.0 0.1 fusion.29
  10.1 199.5 %all-reduce.7.cloned.1.call-done = (f32[2048,128]{1,0:T(8,128)}, f32[2048,128]{1,0:T(8,128)}, f32[2048,128]{1,0:T(8,128)}, f32[2048,128]{1,0:T(8,128)}) async-done(((f32[2048,128]{1,0:T(8,128)}, f32[2048,128]{1,0:T(8,128)}, f32[2048,128]{1,0:T(8,128)}, f32[2048,128]{1,0:T(8,128)}), (f32[2048,128]{1,0:T(8,128)}, f32[2048,128]{1,0:T(8,128)}, f32[2048,128]{1,0:T(8,128)}, ...) | async-done | bytes 4194320 | tf_op jit(solution)/shard_map/psum | solution.py:9
  209.6 0.0 copy-done.3
  209.6 9.8 %broadcast_select_fusion = (f32[2048,512]{1,0:T(8,128)S(1)}, f32[2048,512]{1,0:T(8,128)}) fusion(pred[2048]{0:T(1024)(128)(4,1)S(1)} %get-tuple-element.35, f32[2,512,512]{2,1,0:T(8,128)S(1)} %copy-done.3, f32[2048,128]{1,0:T(8,128)} %get-tuple-element.21, f32[2048,128]{1,0:T(8,128)} %get-tuple-element.22, f32[2048,128]{1,0:T(8,128)} %get-tuple-element.23, ...), kind=kOutput, calls=%fused_computation.20 | convolution fusion | flops 6446645248 | bytes 13633536 | tf_op jit(solution)/shard_map/dot_general | solution.py:13
  219.4 0.0 copy-start
  219.4 0.0 copy-start.2
  219.4 2.0 copy-done
  221.4 1.1 tile.17
  222.5 4.3 all-to-all-start
  226.8 0.0 all-reduce.5.cloned.1.call-start
  226.8 13.7 %all-to-all-done = f32[4,128,512]{2,1,0:T(8,128)S(1)} async-done(((f32[4,128,512]{2,1,0:T(8,128)}), f32[4,128,512]{2,1,0:T(8,128)S(1)}, u32[]{:S(2)}, u32[]{:S(2)}) %all-to-all-start) | async-done | bytes 1048608 | tf_op jit(solution)/shard_map/all_to_all | solution.py:50
  240.5 0.0 copy-done.2
  240.5 8.0 %broadcast_select_fusion.5 = (f32[2048,128]{1,0:T(8,128)}, f32[2048,128]{1,0:T(8,128)}, f32[2048,128]{1,0:T(8,128)}, f32[2048,128]{1,0:T(8,128)}, f32[2048,128]{1,0:T(8,128)S(1)}) fusion(pred[]{:T(512)S(6)} %eq.26, pred[]{:T(512)S(6)} %eq.33, pred[]{:T(512)S(6)} %eq.32, pred[]{:T(512)S(6)} %eq.31, f32[2048,128]{1,0:T(8,128)S(1)} %bitcast.38, ...), kind=kOutput, calls=%fused_computation.31 | convolution fusion | flops 1612447744 | bytes 11798541 | tf_op jit(solution)/shard_map/dot_general | solution.py:13
  248.4 0.0 all-reduce.5.cloned.1.call-update
  248.5 192.9 %all-reduce.5.cloned.1.call-done = (f32[2048,128]{1,0:T(8,128)}, f32[2048,128]{1,0:T(8,128)}, f32[2048,128]{1,0:T(8,128)}, f32[2048,128]{1,0:T(8,128)}) async-done(((f32[2048,128]{1,0:T(8,128)}, f32[2048,128]{1,0:T(8,128)}, f32[2048,128]{1,0:T(8,128)}, f32[2048,128]{1,0:T(8,128)}), (f32[2048,128]{1,0:T(8,128)}, f32[2048,128]{1,0:T(8,128)}, f32[2048,128]{1,0:T(8,128)}, ...) | async-done | bytes 4194320 | tf_op jit(solution)/shard_map/psum | solution.py:9
  441.3 10.3 %broadcast_select_fusion.1 = (f32[2048,512]{1,0:T(8,128)S(1)}, f32[2048,512]{1,0:T(8,128)}) fusion(pred[2048]{0:T(1024)(128)(4,1)S(1)} %get-tuple-element.33, f32[2,512,512]{2,1,0:T(8,128)} %param.5, f32[2048,128]{1,0:T(8,128)} %get-tuple-element.17, f32[2048,128]{1,0:T(8,128)} %get-tuple-element.18, f32[2048,128]{1,0:T(8,128)} %get-tuple-element.19, ...), kind=kOutput, calls=%fused_computation.21 | convolution fusion | flops 6446645248 | bytes 13633536 | tf_op jit(solution)/shard_map/dot_general | solution.py:13
  451.6 0.0 copy-start.1
  451.6 2.0 copy-done.1
  453.6 1.1 tile.19
  454.7 4.3 all-to-all-start.1
  459.0 13.7 %all-to-all-done.1 = f32[4,128,512]{2,1,0:T(8,128)S(1)} async-done(((f32[4,128,512]{2,1,0:T(8,128)}), f32[4,128,512]{2,1,0:T(8,128)S(1)}, u32[]{:S(2)}, u32[]{:S(2)}) %all-to-all-start.1) | async-done | bytes 1048608 | tf_op jit(solution)/shard_map/all_to_all | solution.py:50
  472.7 6.9 %fusion.16 = f32[2048,128]{1,0:T(8,128)} fusion(f32[2048,128]{1,0:T(8,128)S(1)} %get-tuple-element.38, f32[2048,512]{1,0:T(8,128)} %copy-done.1, f32[2048,512]{1,0:T(8,128)} %get-tuple-element.40, s32[]{:T(128)S(6)} %select_n.137, pred[2048]{0:T(1024)(128)(4,1)S(1)} %get-tuple-element.35, pred[]{:T(512)S(6)} %and.21, f32[512,512]{1,0:T(8,128)S(1)} %bitcast.40, ...), kind=kOutput, calls=%fused_computation.17 | convolution fusion | flops 1611399168 | bytes 7604233 | tf_op jit(solution)/shard_map/dot_general | solution.py:13
  (3 shorter events, 0.0 us)
Async XLA Ops:
  6.5 203.1 %all-reduce.7.cloned.1.call-start = ((), (), s32[]{:S(2)}) async-start(), calls=%async_computation.3 | async-start | bytes 8388608 | tf_op jit(solution)/shard_map/psum | solution.py:9
  6.5 203.1 %copy-start.3 = (f32[2,512,512]{2,1,0:T(8,128)S(1)}, f32[2,512,512]{2,1,0:T(8,128)}, u32[]{:S(2)}) copy-start(f32[2,512,512]{2,1,0:T(8,128)} %param.5) | copy-start | bytes 6291460
  219.4 2.0 copy-start
  219.4 21.1 %copy-start.2 = (f32[16,128,1,128]{3,2,1,0:T(1,128)S(1)}, f32[16,128,1,128]{3,2,1,0:T(1,128)}, u32[]{:S(2)}) copy-start(f32[16,128,1,128]{3,2,1,0:T(1,128)} %param.4) | copy-start | bytes 3145732
  222.5 18.0 %all-to-all-start = ((f32[4,128,512]{2,1,0:T(8,128)}), f32[4,128,512]{2,1,0:T(8,128)S(1)}, u32[]{:S(2)}, u32[]{:S(2)}) async-start(f32[4,128,512]{2,1,0:T(8,128)} %tile.17), calls=%async_computation | async-start | bytes 2097152 | tf_op jit(solution)/shard_map/all_to_all | solution.py:50
  226.8 214.5 %all-reduce.5.cloned.1.call-start = ((), (), s32[]{:S(2)}) async-start(), calls=%async_computation.2 | async-start | bytes 8388608 | tf_op jit(solution)/shard_map/psum | solution.py:9
  451.6 2.0 copy-start.1
  454.7 18.0 %all-to-all-start.1 = ((f32[4,128,512]{2,1,0:T(8,128)}), f32[4,128,512]{2,1,0:T(8,128)S(1)}, u32[]{:S(2)}, u32[]{:S(2)}) async-start(f32[4,128,512]{2,1,0:T(8,128)} %tile.19), calls=%async_computation.1 | async-start | bytes 2097152 | tf_op jit(solution)/shard_map/all_to_all | solution.py:50
Sparse Core Ops, SparseCore 0:
  11.3 198.2 all-reduce.6
  248.6 192.6 all-reduce.4
